TPU v7x, 32 devices: a whole 2x2x4 slice. The times are simulated.
32 devices in a mesh: tile: 8 (over y, x, core), depth: 4 (over z).
Axes of the slice: x: 2, y: 2, z: 4, core: 2. Of those that a mesh axis runs over, the one named last changes fastest.
Arguments:
- features: bfloat16 [4, 2048, 128], P('depth', 'tile'), may hold values from -4 to 4
- logits: float32 [4, 2048], P('depth', 'tile'), may hold values from -2.75 to 5.5
- geometry: float32 [2, 4, 5, 2048], P(None, 'depth', None, 'tile'), may hold values from -0.6 to 32, as said below
- dest_slot: int32 [2, 4, 2048], P(None, 'depth', 'tile'), may hold values from -1 to 2047, as said below
- target: bfloat16 [2, 16, 128, 1024], P(None, 'tile'), may hold values from -3 to 3
Outputs:
- images: bfloat16 [2, 16, 128, 1024], P(None, 'tile', None, 'depth')
- new_features: bfloat16 [4, 2048, 128], P('depth', 'tile')
- new_logits: float32 [4, 2048], P('depth', 'tile')
- shape_grads: float32 [2, 4, 5, 2048], P(None, 'depth', None, 'tile')
Inputs may be any that keep to these rules, and one draw needn't show every extreme that they name: `dest_slot`: for each view and layer no two splats share a slot; -1 marks a splat outside the view; a splat's place within its tile is its front-to-back order. At most 32 splats of one layer held by one index of tile go to the tiles of one index of tile, and in every view and layer there is an index of tile whose tiles receive exactly 32 from every owner, so that all their slots are used. `geometry`: components 0 and 1 are a splat's centre in pixels within its tile, from 0 to 32; components 2 and 3 lie in -0.5 to 2.0; component 4 in -0.6 to 0.6.
All inputs are finite; a program needn't handle non-finite values.
Results may differ from a plain program's by a relative error of at most 0.0073.
Values may be sent and summed in bfloat16 or wider, within the bound.
A program may use at most 64 MiB of HBM per device.

v0:
```python
from functools import partial
import jax
import jax.numpy as jnp
from jax import lax
from jax.sharding import PartitionSpec as P

F = 128
W = 32
S = 128
VIEWS = 2
P_SIZE = 1024
clamp_top = 0.99
feature_rate = 0.5
opacity_rate = 0.5


def pixel_places():
    places = jnp.arange(P_SIZE, dtype=jnp.int32)
    across = (places % W).astype(jnp.float32) + 0.5
    downward = (places // W).astype(jnp.float32) + 0.5
    return (across, downward)


def block_sum(values, reverse):
    length = values.shape[0]
    block_rows = min(128, length)
    blocks = values.reshape(length // block_rows, block_rows, values.shape[1])
    positions = jnp.arange(block_rows)
    if reverse:
        triangle = (positions[:, None] < positions[None, :]).astype(jnp.float32)
    else:
        triangle = (positions[:, None] > positions[None, :]).astype(jnp.float32)
    within = jnp.einsum("ij,bjp->bip", triangle, blocks, precision=lax.Precision.HIGHEST)
    block_totals = jnp.sum(blocks, axis=1)
    if reverse:
        offsets = jnp.sum(block_totals, axis=0)[None, :] - jnp.cumsum(block_totals, axis=0)
    else:
        offsets = jnp.cumsum(block_totals, axis=0) - block_totals
    return (within + offsets[:, None, :]).reshape(length, values.shape[1])


def splat_fields(shapes):
    across, downward = pixel_places()
    delta_x = across[None, :] - shapes[0][:, None]
    delta_y = downward[None, :] - shapes[1][:, None]
    coef_a = jnp.exp(shapes[2])[:, None]
    coef_c = jnp.exp(shapes[3])[:, None]
    spread = jnp.exp(0.5 * (shapes[2] + shapes[3]))[:, None]
    coef_b = shapes[4][:, None] * spread
    quadric = (
        coef_a * delta_x * delta_x + 2.0 * coef_b * delta_x * delta_y + coef_c * delta_y * delta_y
    )
    falloff = jnp.exp(-0.5 * quadric)
    opacity = shapes[5][:, None]
    product = opacity * falloff
    coverage = jnp.minimum(product, clamp_top)
    return (delta_x, delta_y, coef_a, coef_b, coef_c, spread, falloff, opacity, product, coverage)


def layer_forward(inputs):
    slot_feats, shapes = inputs
    coverage = splat_fields(shapes)[9]
    log_keep = jnp.log(1.0 - coverage)
    before = block_sum(log_keep, False)
    weights = (coverage * jnp.exp(before)).astype(jnp.bfloat16)
    composite = lax.dot_general(
        slot_feats, weights, (((0,), (0,)), ((), ())), preferred_element_type=jnp.float32
    )
    layer_keep = jnp.exp(jnp.sum(log_keep, axis=0))
    return (composite, layer_keep)


def layer_backward(inputs):
    slot_feats, shapes, grad_comp, grad_keep = inputs
    delta_x, delta_y, coef_a, coef_b, coef_c, spread, falloff, opacity, product, coverage = (
        splat_fields(shapes)
    )
    log_keep = jnp.log(1.0 - coverage)
    before = block_sum(log_keep, False)
    decayed = jnp.exp(before)
    exact_weight = coverage * decayed
    weights = exact_weight.astype(jnp.bfloat16)
    layer_keep = jnp.exp(jnp.sum(log_keep, axis=0))
    grad_feat = lax.dot_general(
        weights, grad_comp, (((1,), (1,)), ((), ())), preferred_element_type=jnp.float32
    )
    grad_weight = jnp.dot(slot_feats, grad_comp, preferred_element_type=jnp.float32)
    grad_before = grad_weight * exact_weight
    later = block_sum(grad_before, True)
    grad_log = later + (grad_keep * layer_keep)[None, :]
    grad_coverage = grad_weight * decayed - grad_log / (1.0 - coverage)
    grad_product = jnp.where(product < clamp_top, grad_coverage, 0.0)
    grad_quadric = -0.5 * opacity * falloff * grad_product
    grad_mean_x = -2.0 * jnp.sum(grad_quadric * (coef_a * delta_x + coef_b * delta_y), axis=1)
    grad_mean_y = -2.0 * jnp.sum(grad_quadric * (coef_b * delta_x + coef_c * delta_y), axis=1)
    grad_first = jnp.sum(grad_quadric * delta_x * delta_x, axis=1)
    grad_cross = jnp.sum(grad_quadric * 2.0 * delta_x * delta_y, axis=1)
    grad_second = jnp.sum(grad_quadric * delta_y * delta_y, axis=1)
    grad_log_a = coef_a[:, 0] * grad_first + 0.5 * coef_b[:, 0] * grad_cross
    grad_log_c = coef_c[:, 0] * grad_second + 0.5 * coef_b[:, 0] * grad_cross
    grad_corr = spread[:, 0] * grad_cross
    opacity_flat = opacity[:, 0]
    grad_logit = opacity_flat * (1.0 - opacity_flat) * jnp.sum(falloff * grad_product, axis=1)
    grad_shape = jnp.stack(
        [grad_mean_x, grad_mean_y, grad_log_a, grad_log_c, grad_corr, grad_logit]
    )
    return (grad_feat, grad_shape)


def rear_step(all_keeps, all_terms, depth_here, layers, counter, carried):
    layer_at = layers - 1 - counter
    updated = all_terms[layer_at] + all_keeps[layer_at] * carried
    return jnp.where(layer_at > depth_here, updated, carried)


def body(features, logits, geometry, dest_slot, target):
    owners = lax.axis_size("tile")
    layers = lax.axis_size("depth")
    depth_here = lax.axis_index("depth")
    tiles_here = target.shape[1]
    owned = features.shape[1]
    capacity = owned // owners
    pixel_share = P_SIZE // layers
    splat_feats = features[0]
    logit_now = logits[0]
    images = []
    shape_grads = []
    for view_index in range(VIEWS):
        slot_ids = dest_slot[view_index, 0]
        visible = slot_ids >= 0
        receiver = jnp.where(visible, slot_ids // owned, owners)
        matches = (receiver[:, None] == jnp.arange(owners, dtype=jnp.int32)[None, :]).astype(
            jnp.int32
        )
        place_in = jnp.sum((jnp.cumsum(matches, axis=0) - matches) * matches, axis=1)
        position = jnp.where(visible, receiver * capacity + place_in, owners * capacity)
        local_slot = jnp.where(visible, slot_ids - receiver * owned, -1)
        opacity = jax.nn.sigmoid(logit_now)
        shape_rows = jnp.concatenate([geometry[view_index, 0], opacity[None, :]], axis=0).T
        row_buffer = (
            jnp.zeros((owners * capacity + 1, F), jnp.bfloat16)
            .at[position]
            .set(splat_feats)[:-1]
            .reshape(owners, capacity, F)
        )
        slot_buffer = (
            jnp.full((owners * capacity + 1,), -1, jnp.int32)
            .at[position]
            .set(local_slot)[:-1]
            .reshape(owners, capacity)
        )
        shape_buffer = (
            jnp.zeros((owners * capacity + 1, 6), jnp.float32)
            .at[position]
            .set(shape_rows)[:-1]
            .reshape(owners, capacity, 6)
        )
        got_rows, got_slots = (
            lax.all_to_all(row_buffer, "tile", split_axis=0, concat_axis=0, tiled=True),
            lax.all_to_all(slot_buffer, "tile", split_axis=0, concat_axis=0, tiled=True),
        )
        got_shapes = lax.all_to_all(shape_buffer, "tile", split_axis=0, concat_axis=0, tiled=True)
        arrived = got_slots.reshape(-1)
        present = arrived >= 0
        landing = jnp.where(present, arrived, owned)
        slot_feats = (
            jnp.zeros((owned + 1, F), jnp.bfloat16)
            .at[landing]
            .set(got_rows.reshape(-1, F))[:-1]
            .reshape(tiles_here, S, F)
        )
        slot_shapes = (
            jnp.zeros((owned + 1, 6), jnp.float32)
            .at[landing]
            .set(got_shapes.reshape(-1, 6))[:-1]
            .reshape(tiles_here, S, 6)
            .transpose(0, 2, 1)
        )
        composites, layer_keeps = lax.map(layer_forward, (slot_feats, slot_shapes))
        all_keeps = lax.all_gather(layer_keeps[None], "depth", axis=0, tiled=True)
        earlier_mask = (jnp.arange(layers) < depth_here)[:, None, None]
        ahead = jnp.prod(jnp.where(earlier_mask, all_keeps, 1.0), axis=0)
        contrib = ahead[:, None, :] * composites
        summed = lax.psum(contrib, "depth")
        residual = summed - target[view_index].astype(jnp.float32)
        image_part = lax.dynamic_slice_in_dim(summed, depth_here * pixel_share, pixel_share, 2)
        images.append(image_part.astype(jnp.bfloat16))
        pixel_terms = jnp.sum(residual * composites, axis=1)
        all_terms = lax.all_gather(pixel_terms[None], "depth", axis=0, tiled=True)
        behind = lax.fori_loop(
            0,
            layers,
            partial(rear_step, all_keeps, all_terms, depth_here, layers),
            jnp.zeros_like(pixel_terms),
        )
        grad_keep = ahead * behind
        grad_comp = (ahead[:, None, :] * residual).astype(jnp.bfloat16)
        grad_feat, grad_shape = lax.map(
            layer_backward, (slot_feats, slot_shapes, grad_comp, grad_keep)
        )
        flat_feat = grad_feat.reshape(owned, F)
        flat_shape = grad_shape.transpose(0, 2, 1).reshape(owned, 6)
        fetched = jnp.where(present, arrived, 0)
        back_feat = jnp.where(present[:, None], flat_feat[fetched], 0.0).reshape(
            owners, capacity, F
        )
        back_shape = jnp.where(present[:, None], flat_shape[fetched], 0.0).reshape(
            owners, capacity, 6
        )
        return_feat, return_shape = (
            lax.all_to_all(back_feat, "tile", split_axis=0, concat_axis=0, tiled=True),
            lax.all_to_all(back_shape, "tile", split_axis=0, concat_axis=0, tiled=True),
        )
        padded_feat = jnp.concatenate(
            [return_feat.reshape(-1, F), jnp.zeros((1, F), jnp.float32)], axis=0
        )
        padded_shape = jnp.concatenate(
            [return_shape.reshape(-1, 6), jnp.zeros((1, 6), jnp.float32)], axis=0
        )
        splat_grad_feat = padded_feat[position]
        splat_grad_shape = padded_shape[position]
        shape_grads.append(splat_grad_shape[:, :5].T)
        splat_feats = (splat_feats.astype(jnp.float32) - feature_rate * splat_grad_feat).astype(
            jnp.bfloat16
        )
        logit_now = logit_now - opacity_rate * splat_grad_shape[:, 5]
    return (jnp.stack(images), splat_feats[None], logit_now[None], jnp.stack(shape_grads)[:, None])


def solution(mesh):
    placed = (
        P("depth", "tile", None),
        P("depth", "tile"),
        P(None, "depth", None, "tile"),
        P(None, "depth", "tile"),
        P(None, "tile", None, None),
    )
    return jax.shard_map(
        body,
        mesh=mesh,
        in_specs=placed,
        out_specs=(
            P(None, "tile", None, "depth"),
            P("depth", "tile", None),
            P("depth", "tile"),
            P(None, "depth", None, "tile"),
        ),
        check_vma=False,
    )
```

profile of v0, /device:TPU:0, one launch (start us, length us, event | category | flops | bytes accessed | tf_op | source)
XLA Modules:
  0.0 308.5 jit_solution(4619955164635074478)
XLA Ops:
  13.0 1.4 scatter_custom_fusion
  15.1 5.3 %all-to-all-start = ((s32[8,1,32]{2,1,0:T(1,128)}), s32[8,1,32]{2,1,0:T(1,128)S(1)}, u32[]{:S(2)}, u32[]{:S(2)}) async-start(s32[8,1,32]{2,1,0:T(1,128)} %all_to_all.36), calls=%async_computation | async-start | bytes 8192 | tf_op jit(solution)/shard_map/all_to_all | solution.py:160
  20.7 1.2 scatter_custom_fusion.3
  22.7 2.4 all-to-all-done
  25.1 3.3 %all-to-all-start.2 = ((f32[8,1,192]{2,1,0:T(1,128)}), f32[8,1,192]{2,1,0:T(1,128)S(1)}, u32[]{:S(2)}, u32[]{:S(2)}) async-start(f32[8,1,192]{2,1,0:T(1,128)} %reshape.3803), calls=%async_computation.2 | async-start | bytes 16384 | tf_op jit(solution)/shard_map/all_to_all | solution.py:162
  28.4 1.2 scatter_custom_fusion.1
  31.5 1.6 all-to-all-done.2
  33.1 3.4 %all-to-all-start.1 = ((bf16[8,32,128]{2,1,0:T(8,128)(2,1)}), bf16[8,32,128]{2,1,0:T(8,128)(2,1)S(1)}, u32[]{:S(2)}, u32[]{:S(2)}) async-start(bf16[8,32,128]{2,1,0:T(8,128)(2,1)} %bitcast.95), calls=%async_computation.1 | async-start | bytes 131072 | tf_op jit(solution)/shard_map/all_to_all | solution.py:159
  39.0 2.4 all-to-all-done.1
  41.4 1.2 scatter_custom_fusion.2
  44.0 5.1 %while.88 = (s32[]{:T(128)}, f32[2,128,1024]{2,1,0:T(8,128)S(1)}, f32[2,1024]{1,0:T(2,128)S(1)}, bf16[2,128,128]{2,1,0:T(8,128)(2,1)S(1)}, f32[2,6,128]{2,1,0:T(8,128)S(1)}, /*index=5*/s32[]{:T(128)}, s32[]{:T(128)}) while((s32[]{:T(128)}, f32[2,128,1024]{2,1,0:T(8,128)S(1)}, f32[2,1024]{1,0:T(2,128)S(1)}, ...), condition=%wide.region_11.12_spmd, body=%wide.region_8.11_spmd.sunk | while | flops 242777600 | bytes 1177693 | solution.py:179
  45.1 1.2 fusion.315
  47.6 1.2 fusion.315
  49.1 13.4 %all-gather.4 = f32[4,2,1024]{2,1,0:T(2,128)S(1)} all-gather(f32[1,2,1024]{2,1,0:T(2,128)S(1)} %bitcast.689), channel_id=2, replica_groups=mesh['tile'=8,'depth'=4] {'depth'}, dimensions={0}, use_global_device_ids=true | all-gather | bytes 40960 | tf_op jit(solution)/shard_map/all_gather | solution.py:180
  63.8 1.4 scatter_custom_fusion.5
  65.9 49.1 %all-reduce.7.cloned.1.call-done = f32[2,128,1024]{2,1,0:T(8,128)} async-done(((f32[2,128,1024]{2,1,0:T(8,128)}), f32[2,128,1024]{2,1,0:T(8,128)}) %all-reduce.7.cloned.1.call-update) | async-done | bytes 1048592 | tf_op jit(solution)/shard_map/psum | solution.py:184
  115.0 1.5 multiply_reduce_fusion.3
  116.5 13.3 %all-gather.5 = f32[4,2,1024]{2,1,0:T(2,128)S(1)} all-gather(f32[1,2,1024]{2,1,0:T(2,128)S(1)} %bitcast.687), channel_id=3, replica_groups=mesh['tile'=8,'depth'=4] {'depth'}, dimensions={0}, use_global_device_ids=true | all-gather | bytes 40960 | tf_op jit(solution)/shard_map/all_gather | solution.py:189
  130.0 9.6 %while.89 = (s32[]{:T(128)}, f32[2,128,128]{2,1,0:T(8,128)S(1)}, f32[2,6,128]{2,1,0:T(8,128)S(1)}, f32[2,6,128]{2,1,0:T(8,128)S(1)}, bf16[2,128,1024]{2,1,0:T(8,...) while((s32[]{:T(128)}, f32[2,128,128]{2,1,0:T(8,128)S(1)}, ...), condition=%wide.region_31.32_spmd, body=%wide.region_21.31_spmd.sunk | while | flops 485672448 | bytes 3947113 | solution.py:198
  132.9 1.9 fusion.325
  137.7 1.9 fusion.325
  142.1 3.7 %all-to-all-start.6 = ((f32[8,1,192]{2,1,0:T(1,128)}), f32[8,1,192]{2,1,0:T(1,128)S(1)}, u32[]{:S(2)}, u32[]{:S(2)}) async-start(f32[8,1,192]{2,1,0:T(1,128)} %reshape.3805), calls=%async_computation.6 | async-start | bytes 16384 | tf_op jit(solution)/shard_map/all_to_all | solution.py:212
  146.5 4.0 %all-to-all-done.6 = f32[8,1,192]{2,1,0:T(1,128)S(1)} async-done(((f32[8,1,192]{2,1,0:T(1,128)}), f32[8,1,192]{2,1,0:T(1,128)S(1)}, u32[]{:S(2)}, u32[]{:S(2)}) %all-to-all-start.6) | async-done | bytes 6176 | tf_op jit(solution)/shard_map/all_to_all | solution.py:212
  150.4 3.3 %all-to-all-start.3 = ((s32[8,1,32]{2,1,0:T(1,128)}), s32[8,1,32]{2,1,0:T(1,128)S(1)}, u32[]{:S(2)}, u32[]{:S(2)}) async-start(s32[8,1,32]{2,1,0:T(1,128)} %all_to_all.40), calls=%async_computation.3 | async-start | bytes 8192 | tf_op jit(solution)/shard_map/all_to_all | solution.py:160
  155.5 2.8 all-to-all-done.3
  158.3 3.4 %all-to-all-start.4 = ((f32[8,32,128]{2,1,0:T(8,128)}), f32[8,32,128]{2,1,0:T(8,128)S(1)}, u32[]{:S(2)}, u32[]{:S(2)}) async-start(f32[8,32,128]{2,1,0:T(8,128)} %broadcast_select_fusion.1), calls=%async_computation.4 | async-start | bytes 262144 | tf_op jit(solution)/shard_map/all_to_all | solution.py:211
  161.9 1.2 scatter_custom_fusion.8
  163.9 3.3 %all-to-all-done.4 = f32[8,32,128]{2,1,0:T(8,128)S(1)} async-done(((f32[8,32,128]{2,1,0:T(8,128)}), f32[8,32,128]{2,1,0:T(8,128)S(1)}, u32[]{:S(2)}, u32[]{:S(2)}) %all-to-all-start.4) | async-done | bytes 131104 | tf_op jit(solution)/shard_map/all_to_all | solution.py:211
  167.1 3.3 %all-to-all-start.7 = ((f32[8,1,192]{2,1,0:T(1,128)}), f32[8,1,192]{2,1,0:T(1,128)S(1)}, u32[]{:S(2)}, u32[]{:S(2)}) async-start(f32[8,1,192]{2,1,0:T(1,128)} %reshape.3807), calls=%async_computation.7 | async-start | bytes 16384 | tf_op jit(solution)/shard_map/all_to_all | solution.py:162
  171.9 1.2 scatter_custom_fusion.6
  173.8 1.3 all-to-all-done.7
  175.1 3.4 %all-to-all-start.5 = ((bf16[8,32,128]{2,1,0:T(8,128)(2,1)}), bf16[8,32,128]{2,1,0:T(8,128)(2,1)S(1)}, u32[]{:S(2)}, u32[]{:S(2)}) async-start(bf16[8,32,128]{2,1,0:T(8,128)(2,1)} %bitcast.121), calls=%async_computation.5 | async-start | bytes 131072 | tf_op jit(solution)/shard_map/all_to_all | solution.py:159
  180.6 2.9 all-to-all-done.5
  183.4 1.2 scatter_custom_fusion.7
  186.1 5.1 %while.90 = (s32[]{:T(128)}, f32[2,128,1024]{2,1,0:T(8,128)S(1)}, f32[2,1024]{1,0:T(2,128)S(1)}, bf16[2,128,128]{2,1,0:T(8,128)(2,1)S(1)}, f32[2,6,128]{2,1,0:T(8,128)S(1)}, /*index=5*/s32[]{:T(128)}, s32[]{:T(128)}) while((s32[]{:T(128)}, f32[2,128,1024]{2,1,0:T(8,128)S(1)}, f32[2,1024]{1,0:T(2,128)S(1)}, ...), condition=%wide.region_39.40_spmd, body=%wide.region_36.39_spmd.sunk | while | flops 242777600 | bytes 1177693 | solution.py:179
  187.1 1.2 fusion.331
  189.7 1.2 fusion.331
  191.2 13.1 %all-gather.6 = f32[4,2,1024]{2,1,0:T(2,128)S(1)} all-gather(f32[1,2,1024]{2,1,0:T(2,128)S(1)} %bitcast.691), channel_id=4, replica_groups=mesh['tile'=8,'depth'=4] {'depth'}, dimensions={0}, use_global_device_ids=true | all-gather | bytes 40960 | tf_op jit(solution)/shard_map/all_gather | solution.py:180
  206.7 48.4 %all-reduce.9.cloned.1.call-done = f32[2,128,1024]{2,1,0:T(8,128)} async-done(((f32[2,128,1024]{2,1,0:T(8,128)}), f32[2,128,1024]{2,1,0:T(8,128)}) %all-reduce.9.cloned.1.call-update) | async-done | bytes 1048592 | tf_op jit(solution)/shard_map/psum | solution.py:184
  255.1 1.5 multiply_reduce_fusion.2
  256.6 13.4 %all-gather.7 = f32[4,2,1024]{2,1,0:T(2,128)S(1)} all-gather(f32[1,2,1024]{2,1,0:T(2,128)S(1)} %bitcast.688), channel_id=5, replica_groups=mesh['tile'=8,'depth'=4] {'depth'}, dimensions={0}, use_global_device_ids=true | all-gather | bytes 40960 | tf_op jit(solution)/shard_map/all_gather | solution.py:189
  270.2 9.7 %while.91 = (s32[]{:T(128)}, f32[2,128,128]{2,1,0:T(8,128)S(1)}, f32[2,6,128]{2,1,0:T(8,128)S(1)}, f32[2,6,128]{2,1,0:T(8,128)S(1)}, bf16[2,128,1024]{2,1,0:T(8,...) while((s32[]{:T(128)}, f32[2,128,128]{2,1,0:T(8,128)S(1)}, ...), condition=%wide.region_55.56_spmd, body=%wide.region_45.55_spmd.sunk | while | flops 485672448 | bytes 3947113 | solution.py:198
  273.0 1.9 fusion.341
  277.9 1.9 fusion.341
  283.0 3.7 %all-to-all-start.9 = ((f32[8,1,192]{2,1,0:T(1,128)}), f32[8,1,192]{2,1,0:T(1,128)S(1)}, u32[]{:S(2)}, u32[]{:S(2)}) async-start(f32[8,1,192]{2,1,0:T(1,128)} %reshape.3809), calls=%async_computation.9 | async-start | bytes 16384 | tf_op jit(solution)/shard_map/all_to_all | solution.py:212
  288.4 3.0 all-to-all-done.9
  291.4 3.4 %all-to-all-start.8 = ((f32[8,32,128]{2,1,0:T(8,128)}), f32[8,32,128]{2,1,0:T(8,128)S(1)}, u32[]{:S(2)}, u32[]{:S(2)}) async-start(f32[8,32,128]{2,1,0:T(8,128)} %broadcast_select_fusion), calls=%async_computation.8 | async-start | bytes 262144 | tf_op jit(solution)/shard_map/all_to_all | solution.py:211
  297.8 2.4 all-to-all-done.8
  (264 shorter events, 55.0 us)
Async XLA Ops:
  8.8 0.6 copy-start.6
  10.2 0.6 copy-start.7
  10.8 0.7 slice-start.2
  11.5 0.7 slice-start.3
  12.3 0.7 copy-start.5
  13.0 7.5 %copy-start.4 = (f32[2,1,5,256]{3,1,2,0:T(1,128)S(1)}, f32[2,1,5,256]{3,1,2,0:T(1,128)}, u32[]{:S(2)}) copy-start(f32[2,1,5,256]{3,1,2,0:T(1,128)} %param.19) | copy-start | bytes 30724
  15.1 5.3 %copy-start.8 = (f32[1,256]{1,0:T(1,128)S(1)}, f32[1,256]{1,0:T(1,128)}, u32[]{:S(2)}) copy-start(f32[1,256]{1,0:T(1,128)} %param.18) | copy-start | bytes 3076
  15.1 9.9 %all-to-all-start = ((s32[8,1,32]{2,1,0:T(1,128)}), s32[8,1,32]{2,1,0:T(1,128)S(1)}, u32[]{:S(2)}, u32[]{:S(2)}) async-start(s32[8,1,32]{2,1,0:T(1,128)} %all_to_all.36), calls=%async_computation | async-start | bytes 8192 | tf_op jit(solution)/shard_map/all_to_all | solution.py:160
  21.9 6.6 %copy-start.3 = (bf16[1,256,128]{2,1,0:T(8,128)(2,1)S(1)}, bf16[1,256,128]{2,1,0:T(8,128)(2,1)}, u32[]{:S(2)}) copy-start(bf16[1,256,128]{2,1,0:T(8,128)(2,1)} %param.17) | copy-start | bytes 196612
  25.1 8.0 %all-to-all-start.2 = ((f32[8,1,192]{2,1,0:T(1,128)}), f32[8,1,192]{2,1,0:T(1,128)S(1)}, u32[]{:S(2)}, u32[]{:S(2)}) async-start(f32[8,1,192]{2,1,0:T(1,128)} %reshape.3803), calls=%async_computation.2 | async-start | bytes 16384 | tf_op jit(solution)/shard_map/all_to_all | solution.py:162
  33.1 8.3 %all-to-all-start.1 = ((bf16[8,32,128]{2,1,0:T(8,128)(2,1)}), bf16[8,32,128]{2,1,0:T(8,128)(2,1)S(1)}, u32[]{:S(2)}, u32[]{:S(2)}) async-start(bf16[8,32,128]{2,1,0:T(8,128)(2,1)} %bitcast.95), calls=%async_computation.1 | async-start | bytes 131072 | tf_op jit(solution)/shard_map/all_to_all | solution.py:159
  36.4 78.5 %all-reduce.7.cloned.1.call-start = ((), (), s32[]{:S(2)}) async-start(), calls=%async_computation.10 | async-start | bytes 2097152 | tf_op jit(solution)/shard_map/psum | solution.py:184
  42.6 0.6 copy-start.2
  43.2 0.8 slice-start.1
  63.8 51.2 %copy-start = (bf16[2,2,128,1024]{3,2,1,0:T(8,128)(2,1)S(1)}, bf16[2,2,128,1024]{3,2,1,0:T(8,128)(2,1)}, u32[]{:S(2)}) copy-start(bf16[2,2,128,1024]{3,2,1,0:T(8,128)(2,1)} %param.21) | copy-start | bytes 3145732
  142.1 8.4 %all-to-all-start.6 = ((f32[8,1,192]{2,1,0:T(1,128)}), f32[8,1,192]{2,1,0:T(1,128)S(1)}, u32[]{:S(2)}, u32[]{:S(2)}) async-start(f32[8,1,192]{2,1,0:T(1,128)} %reshape.3805), calls=%async_computation.6 | async-start | bytes 16384 | tf_op jit(solution)/shard_map/all_to_all | solution.py:212
  150.4 7.9 %all-to-all-start.3 = ((s32[8,1,32]{2,1,0:T(1,128)}), s32[8,1,32]{2,1,0:T(1,128)S(1)}, u32[]{:S(2)}, u32[]{:S(2)}) async-start(s32[8,1,32]{2,1,0:T(1,128)} %all_to_all.40), calls=%async_computation.3 | async-start | bytes 8192 | tf_op jit(solution)/shard_map/all_to_all | solution.py:160
  158.3 8.8 %all-to-all-start.4 = ((f32[8,32,128]{2,1,0:T(8,128)}), f32[8,32,128]{2,1,0:T(8,128)S(1)}, u32[]{:S(2)}, u32[]{:S(2)}) async-start(f32[8,32,128]{2,1,0:T(8,128)} %broadcast_select_fusion.1), calls=%async_computation.4 | async-start | bytes 262144 | tf_op jit(solution)/shard_map/all_to_all | solution.py:211
  167.1 8.0 %all-to-all-start.7 = ((f32[8,1,192]{2,1,0:T(1,128)}), f32[8,1,192]{2,1,0:T(1,128)S(1)}, u32[]{:S(2)}, u32[]{:S(2)}) async-start(f32[8,1,192]{2,1,0:T(1,128)} %reshape.3807), calls=%async_computation.7 | async-start | bytes 16384 | tf_op jit(solution)/shard_map/all_to_all | solution.py:162
  175.1 8.3 %all-to-all-start.5 = ((bf16[8,32,128]{2,1,0:T(8,128)(2,1)}), bf16[8,32,128]{2,1,0:T(8,128)(2,1)S(1)}, u32[]{:S(2)}, u32[]{:S(2)}) async-start(bf16[8,32,128]{2,1,0:T(8,128)(2,1)} %bitcast.121), calls=%async_computation.5 | async-start | bytes 131072 | tf_op jit(solution)/shard_map/all_to_all | solution.py:159
  178.5 76.6 %all-reduce.9.cloned.1.call-start = ((), (), s32[]{:S(2)}) async-start(), calls=%async_computation.11 | async-start | bytes 2097152 | tf_op jit(solution)/shard_map/psum | solution.py:184
  184.6 0.6 copy-start.1
  185.2 0.8 slice-start
  283.0 8.4 %all-to-all-start.9 = ((f32[8,1,192]{2,1,0:T(1,128)}), f32[8,1,192]{2,1,0:T(1,128)S(1)}, u32[]{:S(2)}, u32[]{:S(2)}) async-start(f32[8,1,192]{2,1,0:T(1,128)} %reshape.3809), calls=%async_computation.9 | async-start | bytes 16384 | tf_op jit(solution)/shard_map/all_to_all | solution.py:212
  291.4 8.8 %all-to-all-start.8 = ((f32[8,32,128]{2,1,0:T(8,128)}), f32[8,32,128]{2,1,0:T(8,128)S(1)}, u32[]{:S(2)}, u32[]{:S(2)}) async-start(f32[8,32,128]{2,1,0:T(8,128)} %broadcast_select_fusion), calls=%async_computation.8 | async-start | bytes 262144 | tf_op jit(solution)/shard_map/all_to_all | solution.py:211
Sparse Core Ops, SparseCore 0:
  63.9 51.0 all-reduce.6
  205.7 49.3 all-reduce.8
where the time goes:
time: 310 us; the launch traced here: 308 us
  waiting for transfers between devices  123 us (40%)
  blocking collectives  53.2 us (17%)
  starting transfers between devices  36.2 us (12%)
  local copies, waits for them, and re-layouts  35.9 us (12%)
  matrix products  22.2 us (7%)
  other arithmetic  21.8 us (7%)
  between operations  14.7 us (5%)
    psum x2, waiting for transfers between devices, body(): summed = lax.psum(contrib, 'depth')  97.4 us
    all_gather x2, blocking collectives, body(): all_terms = lax.all_gather(pixel_terms[None], 'depth', axis=0, tiled=True)  26.7 us
    all_gather x2, blocking collectives, body(): all_keeps = lax.all_gather(layer_keeps[None], 'depth', axis=0, tiled=True)  26.5 us
    dot_general x12, matrix products, block_sum(): jnp.einsum('ij,bjp->bip', triangle, blocks, precision=lax.Precision.HIGHEST)  15.4 us
    all_to_all x2, starting transfers between devices, body(): lax.all_to_all(slot_buffer, 'tile', split_axis=0, concat_axis=0, tiled=True)  8.64 us
    all_to_all x2, starting transfers between devices, body(): lax.all_to_all(back_shape, 'tile', split_axis=0, concat_axis=0, tiled=True)  7.32 us
    all_to_all x2, waiting for transfers between devices, body(): lax.all_to_all(back_shape, 'tile', split_axis=0, concat_axis=0, tiled=True)  6.97 us
    unnamed x28, local copies, waits for them, and re-layouts  6.8 us
  transfers between devices with their start and end apart: 12, of which 12 were waited for; matrix products, arithmetic and copies ran while one was open for 8% of the time, Pallas kernels for 0%

commit v1 on v0

--- a/solution.py
+++ b/solution.py
@@ -181,7 +181,9 @@
         earlier_mask = (jnp.arange(layers) < depth_here)[:, None, None]
         ahead = jnp.prod(jnp.where(earlier_mask, all_keeps, 1.0), axis=0)
         contrib = ahead[:, None, :] * composites
-        summed = lax.psum(contrib, "depth")
+        summed = contrib
+        for hop in (1, 2):
+            summed = summed + lax.ppermute(summed, "depth", [(dev, dev ^ hop) for dev in range(4)])
         residual = summed - target[view_index].astype(jnp.float32)
         image_part = lax.dynamic_slice_in_dim(summed, depth_here * pixel_share, pixel_share, 2)
         images.append(image_part.astype(jnp.bfloat16))

time: 310 us -> 336 us (1.084)
  waiting for transfers between devices: 123 us -> 139 us
  between operations: 14.7 us -> 1.41 us
  local copies, waits for them, and re-layouts: 35.9 us -> 44.2 us
  other arithmetic: 21.8 us -> 28.5 us
  starting transfers between devices: 36.2 us -> 42.3 us
    ppermute x0 -> x4, waiting for transfers between devices: none -> 119 us  [body(): lax.ppermute(summed, 'depth', [(dev, dev ^ hop) for dev in range(4)])]
    psum x2 -> x0, waiting for transfers between devices: 97.4 us -> none  [body(): summed = lax.psum(contrib, 'depth')]
    ppermute x0 -> x4, starting transfers between devices: none -> 7 us  [body(): lax.ppermute(summed, 'depth', [(dev, dev ^ hop) for dev in range(4)])]
    unnamed x28 -> x62, local copies, waits for them, and re-layouts: 6.8 us -> 13.2 us
  transfers between devices with their start and end apart: 12 -> 14, of which waited for: 12 -> 14; matrix products, arithmetic and copies ran while one was open for 8% -> 9% of each run, Pallas kernels for 0% -> 0%
where the time goes in v1:
time: 336 us; the launch traced here: 334 us
  waiting for transfers between devices  139 us (41%)
  blocking collectives  53.6 us (16%)
  local copies, waits for them, and re-layouts  44.2 us (13%)
  starting transfers between devices  42.3 us (13%)
  other arithmetic  28.5 us (8%)
  matrix products  24.2 us (7%)
    ppermute x4, waiting for transfers between devices, body(): lax.ppermute(summed, 'depth', [(dev, dev ^ hop) for dev in range(4)])  119 us
    all_gather x2, blocking collectives, body(): all_keeps = lax.all_gather(layer_keeps[None], 'depth', axis=0, tiled=True)  27.1 us
    all_gather x2, blocking collectives, body(): all_terms = lax.all_gather(pixel_terms[None], 'depth', axis=0, tiled=True)  26.5 us
    dot_general x12, matrix products, block_sum(): jnp.einsum('ij,bjp->bip', triangle, blocks, precision=lax.Precision.HIGHEST)  15.4 us
    unnamed x62, local copies, waits for them, and re-layouts  13.2 us
    all_to_all x2, starting transfers between devices, body(): lax.all_to_all(slot_buffer, 'tile', split_axis=0, concat_axis=0, tiled=True)  8.51 us
    ppermute x4, starting transfers between devices, body(): lax.ppermute(summed, 'depth', [(dev, dev ^ hop) for dev in range(4)])  7 us
    all_to_all x2, starting transfers between devices, body(): lax.all_to_all(back_feat, 'tile', split_axis=0, concat_axis=0, tiled=True)  6.74 us
  transfers between devices with their start and end apart: 14, of which 14 were waited for; matrix products, arithmetic and copies ran while one was open for 9% of the time, Pallas kernels for 0%

profile of v1, /device:TPU:0, one launch (start us, length us, event | category | flops | bytes accessed | tf_op | source)
XLA Modules:
  0.0 334.3 jit_solution(16213645440801537066)
XLA Ops:
  6.5 1.4 scatter_custom_fusion
  8.6 5.2 %all-to-all-start = ((s32[8,1,32]{2,1,0:T(1,128)}), s32[8,1,32]{2,1,0:T(1,128)S(1)}, u32[]{:S(2)}, u32[]{:S(2)}) async-start(s32[8,1,32]{2,1,0:T(1,128)} %all_to_all.36), calls=%async_computation | async-start | bytes 8192 | tf_op jit(solution)/shard_map/all_to_all | solution.py:160
  16.7 1.8 all-to-all-done
  18.4 3.3 all-to-all-start.2
  24.9 1.5 all-to-all-done.2
  26.4 3.4 %all-to-all-start.1 = ((bf16[8,32,128]{2,1,0:T(8,128)(2,1)}), bf16[8,32,128]{2,1,0:T(8,128)(2,1)S(1)}, u32[]{:S(2)}, u32[]{:S(2)}) async-start(bf16[8,32,128]{2,1,0:T(8,128)(2,1)} %bitcast.95), calls=%async_computation.1 | async-start | bytes 131072 | tf_op jit(solution)/shard_map/all_to_all | solution.py:159
  32.4 2.3 all-to-all-done.1
  37.4 5.1 %while.88 = (s32[]{:T(128)}, f32[2,128,1024]{2,1,0:T(8,128)S(1)}, f32[2,1024]{1,0:T(2,128)S(1)}, bf16[2,128,128]{2,1,0:T(8,128)(2,1)S(1)}, f32[2,6,128]{2,1,0:T(8,128)S(1)}, /*index=5*/s32[]{:T(128)}, s32[]{:T(128)}) while((s32[]{:T(128)}, f32[2,128,1024]{2,1,0:T(8,128)S(1)}, f32[2,1024]{1,0:T(2,128)S(1)}, ...), condition=%wide.region_11.12_spmd, body=%wide.region_8.11_spmd.sunk | while | flops 242777600 | bytes 1177685 | solution.py:179
  42.5 13.4 %all-gather.4 = f32[4,2,1024]{2,1,0:T(2,128)S(1)} all-gather(f32[1,2,1024]{2,1,0:T(2,128)S(1)} %bitcast.679), channel_id=2, replica_groups=mesh['tile'=8,'depth'=4] {'depth'}, dimensions={0}, use_global_device_ids=true | all-gather | bytes 40960 | tf_op jit(solution)/shard_map/all_gather | solution.py:180
  56.1 1.6 collective-permute-start
  57.8 21.6 %collective-permute-done = f32[2,128,1024]{2,1,0:T(8,128)S(1)} collective-permute-done((f32[2,128,1024]{2,1,0:T(8,128)S(1)}, f32[2,128,1024]{2,1,0:T(8,128)S(1)}, u32[]{:S(2)}, u32[]{:S(2)}) %collective-permute-start) | collective-permute-done | bytes 1048608 | tf_op jit(solution)/shard_map/ppermute | solution.py:186
  79.6 1.7 collective-permute-start.1
  81.3 1.4 scatter_custom_fusion.5
  83.4 39.5 %collective-permute-done.1 = f32[2,128,1024]{2,1,0:T(8,128)} collective-permute-done((f32[2,128,1024]{2,1,0:T(8,128)S(1)}, f32[2,128,1024]{2,1,0:T(8,128)}, u32[]{:S(2)}, u32[]{:S(2)}) %collective-permute-start.1) | collective-permute-done | bytes 1048608 | tf_op jit(solution)/shard_map/ppermute | solution.py:186
  122.8 1.9 multiply_reduce_fusion.3
  124.8 13.3 %all-gather.5 = f32[4,2,1024]{2,1,0:T(2,128)S(1)} all-gather(f32[1,2,1024]{2,1,0:T(2,128)S(1)} %bitcast.678), channel_id=3, replica_groups=mesh['tile'=8,'depth'=4] {'depth'}, dimensions={0}, use_global_device_ids=true | all-gather | bytes 40960 | tf_op jit(solution)/shard_map/all_gather | solution.py:191
  138.5 11.8 %while.89 = (s32[]{:T(128)}, f32[2,128,128]{2,1,0:T(8,128)S(1)}, f32[2,6,128]{2,1,0:T(8,128)S(1)}, f32[2,6,128]{2,1,0:T(8,128)S(1)}, bf16[2,128,1024]{2,1,0:T(8,...) while((s32[]{:T(128)}, f32[2,128,128]{2,1,0:T(8,128)S(1)}, ...), condition=%wide.region_30.31_spmd, body=%wide.region_20.30_spmd.sunk | while | flops 485672448 | bytes 6044285 | solution.py:200
  140.8 1.9 fusion.327
  142.7 1.6 fusion.325
  146.6 1.9 fusion.327
  148.6 1.6 fusion.325
  152.0 3.3 all-to-all-start.6
  156.8 3.2 all-to-all-done.6
  160.0 3.3 all-to-all-start.3
  165.1 2.8 all-to-all-done.3
  167.8 3.4 %all-to-all-start.4 = ((f32[8,32,128]{2,1,0:T(8,128)}), f32[8,32,128]{2,1,0:T(8,128)S(1)}, u32[]{:S(2)}, u32[]{:S(2)}) async-start(f32[8,32,128]{2,1,0:T(8,128)} %broadcast_select_fusion.1), calls=%async_computation.4 | async-start | bytes 262144 | tf_op jit(solution)/shard_map/all_to_all | solution.py:213
  174.6 2.0 all-to-all-done.4
  176.6 3.3 all-to-all-start.7
  181.5 1.3 scatter_custom_fusion.6
  184.6 3.4 %all-to-all-start.5 = ((bf16[8,32,128]{2,1,0:T(8,128)(2,1)}), bf16[8,32,128]{2,1,0:T(8,128)(2,1)S(1)}, u32[]{:S(2)}, u32[]{:S(2)}) async-start(bf16[8,32,128]{2,1,0:T(8,128)(2,1)} %bitcast.121), calls=%async_computation.5 | async-start | bytes 131072 | tf_op jit(solution)/shard_map/all_to_all | solution.py:159
  190.7 2.3 all-to-all-done.5
  195.6 7.6 %while.90 = (s32[]{:T(128)}, f32[2,128,1024]{2,1,0:T(8,128)S(1)}, f32[2,1024]{1,0:T(2,128)}, bf16[2,128,128]{2,1,0:T(8,128)(2,1)S(1)}, f32[2,6,128]{2,1,0:T(8,128)S(1)}, /*index=5*/s32[]{:T(128)}, s32[]{:T(128)}) while((s32[]{:T(128)}, f32[2,128,1024]{2,1,0:T(8,128)S(1)}, f32[2,1024]{1,0:T(2,128)}, bf16[2,128,128]{2,1,0:T(8,128)(2,1)S(1)}, ...), condition=%wide.region_38.39_spmd, body=%wide.region_35.38_spmd.sunk | while | flops 242777600 | bytes 1177685 | solution.py:179
  198.1 1.3 dynamic_update_slice.71
  201.9 1.3 dynamic_update_slice.71
  203.2 13.7 %all-gather.6 = f32[4,2,1024]{2,1,0:T(2,128)S(1)} all-gather(f32[1,2,1024]{2,1,0:T(2,128)} %bitcast.681), channel_id=4, replica_groups=mesh['tile'=8,'depth'=4] {'depth'}, dimensions={0}, use_global_device_ids=true | all-gather | bytes 40960 | tf_op jit(solution)/shard_map/all_gather | solution.py:180
  217.6 1.6 collective-permute-start.2
  219.2 20.3 %collective-permute-done.2 = f32[2,128,1024]{2,1,0:T(8,128)S(1)} collective-permute-done((f32[2,128,1024]{2,1,0:T(8,128)S(1)}, f32[2,128,1024]{2,1,0:T(8,128)S(1)}, u32[]{:S(2)}, u32[]{:S(2)}) %collective-permute-start.2) | collective-permute-done | bytes 1048608 | tf_op jit(solution)/shard_map/ppermute | solution.py:186
  240.7 2.1 collective-permute-start.3
  247.3 38.0 %collective-permute-done.3 = f32[2,128,1024]{2,1,0:T(8,128)} collective-permute-done((f32[2,128,1024]{2,1,0:T(8,128)}, f32[2,128,1024]{2,1,0:T(8,128)}, u32[]{:S(2)}, u32[]{:S(2)}) %collective-permute-start.3) | collective-permute-done | bytes 1048608 | tf_op jit(solution)/shard_map/ppermute | solution.py:186
  285.4 1.9 multiply_reduce_fusion.2
  287.5 13.2 %all-gather.7 = f32[4,2,1024]{2,1,0:T(2,128)S(1)} all-gather(f32[1,2,1024]{2,1,0:T(2,128)S(1)} %bitcast.677), channel_id=5, replica_groups=mesh['tile'=8,'depth'=4] {'depth'}, dimensions={0}, use_global_device_ids=true | all-gather | bytes 40960 | tf_op jit(solution)/shard_map/all_gather | solution.py:191
  300.7 2.9 while.93
  303.7 9.6 %while.91 = (s32[]{:T(128)}, f32[2,128,128]{2,1,0:T(8,128)S(1)}, f32[2,6,128]{2,1,0:T(8,128)S(1)}, f32[2,6,128]{2,1,0:T(8,128)S(1)}, bf16[2,128,1024]{2,1,0:T(8,...) while((s32[]{:T(128)}, f32[2,128,128]{2,1,0:T(8,128)S(1)}, ...), condition=%wide.region_53.54_spmd, body=%wide.region_43.53_spmd.sunk | while | flops 485672448 | bytes 3947105 | solution.py:200
  305.9 1.9 fusion.343
  310.7 1.9 fusion.343
  316.0 3.3 all-to-all-start.9
  321.8 2.3 all-to-all-done.9
  324.0 3.4 %all-to-all-start.8 = ((f32[8,32,128]{2,1,0:T(8,128)}), f32[8,32,128]{2,1,0:T(8,128)S(1)}, u32[]{:S(2)}, u32[]{:S(2)}) async-start(f32[8,32,128]{2,1,0:T(8,128)} %broadcast_select_fusion), calls=%async_computation.8 | async-start | bytes 262144 | tf_op jit(solution)/shard_map/all_to_all | solution.py:213
  (308 shorter events, 77.3 us)
Async XLA Ops:
  2.2 0.6 copy-start.16
  3.7 0.6 copy-start.17
  4.3 0.7 slice-start.2
  5.0 0.7 slice-start.3
  5.8 0.7 copy-start.15
  6.5 166.1 %copy-start.19 = (s32[256,1]{0,1:T(1,128)}, s32[256,1]{0,1:T(1,128)S(1)}, u32[]{:S(2)}) copy-start(s32[256,1]{0,1:T(1,128)S(1)} %get-tuple-element.807) | copy-start | bytes 3076
  6.5 7.3 %copy-start.11 = (f32[2,1,5,256]{3,1,2,0:T(1,128)S(1)}, f32[2,1,5,256]{3,1,2,0:T(1,128)}, u32[]{:S(2)}) copy-start(f32[2,1,5,256]{3,1,2,0:T(1,128)} %param.19) | copy-start | bytes 30724
  8.6 9.8 %all-to-all-start = ((s32[8,1,32]{2,1,0:T(1,128)}), s32[8,1,32]{2,1,0:T(1,128)S(1)}, u32[]{:S(2)}, u32[]{:S(2)}) async-start(s32[8,1,32]{2,1,0:T(1,128)} %all_to_all.36), calls=%async_computation | async-start | bytes 8192 | tf_op jit(solution)/shard_map/all_to_all | solution.py:160
  13.8 0.7 copy-start.22
  16.0 5.8 %copy-start.4 = (bf16[1,256,128]{2,1,0:T(8,128)(2,1)S(1)}, bf16[1,256,128]{2,1,0:T(8,128)(2,1)}, u32[]{:S(2)}) copy-start(bf16[1,256,128]{2,1,0:T(8,128)(2,1)} %param.17) | copy-start | bytes 196612
  18.4 8.0 %all-to-all-start.2 = ((f32[8,1,192]{2,1,0:T(1,128)}), f32[8,1,192]{2,1,0:T(1,128)S(1)}, u32[]{:S(2)}, u32[]{:S(2)}) async-start(f32[8,1,192]{2,1,0:T(1,128)} %reshape.3803), calls=%async_computation.2 | async-start | bytes 16384 | tf_op jit(solution)/shard_map/all_to_all | solution.py:162
  21.8 34.1 %copy-start.24 = (pred[4]{0:T(512)(128)(4,1)}, pred[4]{0:T(512)(128)(4,1)S(1)}, u32[]{:S(2)}) copy-start(pred[4]{0:T(512)(128)(4,1)S(1)} %iota_compare_fusion.16) | copy-start | bytes 16
  26.4 8.3 %all-to-all-start.1 = ((bf16[8,32,128]{2,1,0:T(8,128)(2,1)}), bf16[8,32,128]{2,1,0:T(8,128)(2,1)S(1)}, u32[]{:S(2)}, u32[]{:S(2)}) async-start(bf16[8,32,128]{2,1,0:T(8,128)(2,1)} %bitcast.95), calls=%async_computation.1 | async-start | bytes 131072 | tf_op jit(solution)/shard_map/all_to_all | solution.py:159
  35.9 0.6 copy-start.3
  36.5 0.8 slice-start.1
  56.1 66.7 %copy-start = (bf16[2,2,128,1024]{3,2,1,0:T(8,128)(2,1)S(1)}, bf16[2,2,128,1024]{3,2,1,0:T(8,128)(2,1)}, u32[]{:S(2)}) copy-start(bf16[2,2,128,1024]{3,2,1,0:T(8,128)(2,1)} %param.21) | copy-start | bytes 3145732
  56.1 23.2 %collective-permute-start = (f32[2,128,1024]{2,1,0:T(8,128)S(1)}, f32[2,128,1024]{2,1,0:T(8,128)S(1)}, u32[]{:S(2)}, u32[]{:S(2)}) collective-permute-start(f32[2,128,1024]{2,1,0:T(8,128)S(1)} %broadcast_multiply_fusion.5), channel_id=1, source_target_pairs={{0,1},{1,0},{2,3},{3,2},{4,5},{5,4},{6,7},{7,6},{8,9},{9,8},{10,11... | collective-permute-start | bytes 3145736 | tf_op jit(solution)/shard_map/ppermute | solution.py:186
  79.6 3.8 %copy-start.1 = (f32[2,128,1024]{2,1,0:T(8,128)}, f32[2,128,1024]{2,1,0:T(8,128)S(1)}, u32[]{:S(2)}) copy-start(f32[2,128,1024]{2,1,0:T(8,128)S(1)} %fusion.278) | copy-start | bytes 3145732
  79.6 43.2 %collective-permute-start.1 = (f32[2,128,1024]{2,1,0:T(8,128)S(1)}, f32[2,128,1024]{2,1,0:T(8,128)}, u32[]{:S(2)}, u32[]{:S(2)}) collective-permute-start(f32[2,128,1024]{2,1,0:T(8,128)S(1)} %fusion.278), channel_id=1, source_target_pairs={{0,2},{1,3},{2,0},{3,1},{4,6},{5,7},{6,4},{7,5},{8,10},{9,11},{10,... | collective-permute-start | bytes 3145736 | tf_op jit(solution)/shard_map/ppermute | solution.py:186
  139.8 0.9 copy-start.26
  145.7 0.9 copy-start.26
  152.0 8.0 %all-to-all-start.6 = ((f32[8,1,192]{2,1,0:T(1,128)}), f32[8,1,192]{2,1,0:T(1,128)S(1)}, u32[]{:S(2)}, u32[]{:S(2)}) async-start(f32[8,1,192]{2,1,0:T(1,128)} %reshape.3805), calls=%async_computation.6 | async-start | bytes 16384 | tf_op jit(solution)/shard_map/all_to_all | solution.py:214
  160.0 7.9 %all-to-all-start.3 = ((s32[8,1,32]{2,1,0:T(1,128)}), s32[8,1,32]{2,1,0:T(1,128)S(1)}, u32[]{:S(2)}, u32[]{:S(2)}) async-start(s32[8,1,32]{2,1,0:T(1,128)} %all_to_all.40), calls=%async_computation.3 | async-start | bytes 8192 | tf_op jit(solution)/shard_map/all_to_all | solution.py:160
  167.8 8.8 %all-to-all-start.4 = ((f32[8,32,128]{2,1,0:T(8,128)}), f32[8,32,128]{2,1,0:T(8,128)S(1)}, u32[]{:S(2)}, u32[]{:S(2)}) async-start(f32[8,32,128]{2,1,0:T(8,128)} %broadcast_select_fusion.1), calls=%async_computation.4 | async-start | bytes 262144 | tf_op jit(solution)/shard_map/all_to_all | solution.py:213
  171.2 0.7 copy-start.23
  176.6 8.0 %all-to-all-start.7 = ((f32[8,1,192]{2,1,0:T(1,128)}), f32[8,1,192]{2,1,0:T(1,128)S(1)}, u32[]{:S(2)}, u32[]{:S(2)}) async-start(f32[8,1,192]{2,1,0:T(1,128)} %reshape.3807), calls=%async_computation.7 | async-start | bytes 16384 | tf_op jit(solution)/shard_map/all_to_all | solution.py:162
  184.6 8.3 %all-to-all-start.5 = ((bf16[8,32,128]{2,1,0:T(8,128)(2,1)}), bf16[8,32,128]{2,1,0:T(8,128)(2,1)S(1)}, u32[]{:S(2)}, u32[]{:S(2)}) async-start(bf16[8,32,128]{2,1,0:T(8,128)(2,1)} %bitcast.121), calls=%async_computation.5 | async-start | bytes 131072 | tf_op jit(solution)/shard_map/all_to_all | solution.py:159
  194.1 0.6 copy-start.2
  194.8 0.8 slice-start
  203.2 13.7 %copy-start.25 = (pred[4]{0:T(512)(128)(4,1)S(1)}, pred[4]{0:T(512)(128)(4,1)}, u32[]{:S(2)}) copy-start(pred[4]{0:T(512)(128)(4,1)} %copy-done.24) | copy-start | bytes 16
  216.9 0.6 copy-start.6
  217.5 22.0 %copy-start.8 = (f32[2,1024]{1,0:T(2,128)}, f32[2,1024]{1,0:T(2,128)S(1)}, u32[]{:S(2)}) copy-start(f32[2,1024]{1,0:T(2,128)S(1)} %select_reduce_fusion) | copy-start | bytes 24580
  217.6 21.9 %collective-permute-start.2 = (f32[2,128,1024]{2,1,0:T(8,128)S(1)}, f32[2,128,1024]{2,1,0:T(8,128)S(1)}, u32[]{:S(2)}, u32[]{:S(2)}) collective-permute-start(f32[2,128,1024]{2,1,0:T(8,128)S(1)} %broadcast_multiply_fusion.4), channel_id=1, source_target_pairs={{0,1},{1,0},{2,3},{3,2},{4,5},{5,4},{6,7},{7,6},{8,9},{9,8},{10,11... | collective-permute-start | bytes 3145736 | tf_op jit(solution)/shard_map/ppermute | solution.py:186
  240.7 44.6 %collective-permute-start.3 = (f32[2,128,1024]{2,1,0:T(8,128)}, f32[2,128,1024]{2,1,0:T(8,128)}, u32[]{:S(2)}, u32[]{:S(2)}) collective-permute-start(f32[2,128,1024]{2,1,0:T(8,128)} %fusion.277), channel_id=1, source_target_pairs={{0,2},{1,3},{2,0},{3,1},{4,6},{5,7},{6,4},{7,5},{8,10},{9,11},{10,... | collective-permute-start | bytes 3145736 | tf_op jit(solution)/shard_map/ppermute | solution.py:186
  242.9 0.7 copy-start.20
  244.1 0.7 copy-start.18
  247.3 40.0 %copy-start.9 = (f32[2,1024]{1,0:T(2,128)S(1)}, f32[2,1024]{1,0:T(2,128)}, u32[]{:S(2)}) copy-start(f32[2,1024]{1,0:T(2,128)} %copy-done.8) | copy-start | bytes 24580
  287.5 13.2 %copy-start.7 = (f32[2,1024]{1,0:T(2,128)S(1)}, f32[2,1024]{1,0:T(2,128)}, u32[]{:S(2)}) copy-start(f32[2,1024]{1,0:T(2,128)} %custom-call.1) | copy-start | bytes 24580
  313.3 0.7 copy-start.14
  314.7 0.7 copy-start.12
  316.0 8.0 %all-to-all-start.9 = ((f32[8,1,192]{2,1,0:T(1,128)}), f32[8,1,192]{2,1,0:T(1,128)S(1)}, u32[]{:S(2)}, u32[]{:S(2)}) async-start(f32[8,1,192]{2,1,0:T(1,128)} %reshape.3809), calls=%async_computation.9 | async-start | bytes 16384 | tf_op jit(solution)/shard_map/all_to_all | solution.py:214
  320.1 0.9 copy-start.5
  324.0 8.8 %all-to-all-start.8 = ((f32[8,32,128]{2,1,0:T(8,128)}), f32[8,32,128]{2,1,0:T(8,128)S(1)}, u32[]{:S(2)}, u32[]{:S(2)}) async-start(f32[8,32,128]{2,1,0:T(8,128)} %broadcast_select_fusion), calls=%async_computation.8 | async-start | bytes 262144 | tf_op jit(solution)/shard_map/all_to_all | solution.py:213
  328.3 0.7 copy-start.13
  329.7 0.7 copy-start.10
  331.2 0.7 copy-start.21
